TPU v7x, 256 devices: a whole 4x4x8 slice. The times are simulated.
256 devices in a mesh: row: 16 (over x, z_lo), col: 16 (over y, z_hi, core).
Axes of the slice: x: 4, y: 4, z: 8 (z_hi: 2, z_lo: 4; z = z_hi * 4 + z_lo), core: 2. Of those that a mesh axis runs over, the one named last changes fastest.
Arguments:
- potential: float32 [32, 64, 512], P('row', 'col'), may hold values from -6 to 6
- basis: bfloat16 [32, 64, 384, 512], P('row', 'col'), may hold values from -6 to 6
- hamiltonian: bfloat16 [6144, 6144], P('row', 'col'), may hold values from -0.078125 to 0.078125
- density: bfloat16 [2, 6144, 6144], P(None, 'row', 'col'), may hold values from -6 to 6
- hmask: int32 [48, 48], replicated, may hold values from 0 to 1, as said below
- pmask: int32 [48, 48], replicated, may hold values from 0 to 1, as said below
Outputs:
- propagated: bfloat16 [2, 6144, 6144], P(None, 'row', 'col')
Inputs may be any that keep to these rules, and one draw needn't show every extreme that they name: hmask[I, I] is always 1; every other block is 1 with probability 1/2, independently. pmask follows the same law as hmask, drawn independently.
All inputs are finite; a program needn't handle non-finite values.
Results may differ from a plain program's by a relative error of at most 0.0062.
Values may be sent and summed in bfloat16 or wider, within the bound.
A program may use at most 64 MiB of HBM per device.

v0:
```python
import jax
import jax.numpy as jnp
from jax import lax
from jax.sharding import PartitionSpec as P

BLK = 128
KAPPA = 0.4
TIME_STEP = 0.5


def extended_2(block, sides, width):
    for axis, dim in sides:
        count = lax.axis_size(axis)
        forward = [(i, i + 1) for i in range(count - 1)]
        backward = [(target, source) for source, target in forward]
        low = lax.ppermute(
            lax.slice_in_dim(block, block.shape[dim] - width, None, axis=dim), axis, forward
        )
        high = lax.ppermute(lax.slice_in_dim(block, 0, width, axis=dim), axis, backward)
        block = jnp.concatenate([low, block, high], axis=dim)
    return block


def shards(potential, basis, hamiltonian, density, hmask, pmask):
    width_x, width_y, depth_z = potential.shape
    extended = extended_2(potential, (("row", 0), ("col", 1)), 1)
    padded = jnp.pad(extended, ((0, 0), (0, 0), (1, 1)))
    beside = padded[2:, 1:-1, 1:-1] + padded[:-2, 1:-1, 1:-1]
    beside = beside + padded[1:-1, 2:, 1:-1] + padded[1:-1, :-2, 1:-1]
    beside = beside + padded[1:-1, 1:-1, 2:] + padded[1:-1, 1:-1, :-2]
    effective = potential + KAPPA * (beside - 6.0 * potential)
    blocks_here = basis.shape[2] // BLK
    weighted = (basis * effective[:, :, None, :]).astype(jnp.bfloat16)
    partial_blocks = jnp.einsum(
        "xykaz,xykbz->kab",
        weighted.reshape(width_x, width_y, blocks_here, BLK, depth_z),
        basis.reshape(width_x, width_y, blocks_here, BLK, depth_z),
        preferred_element_type=jnp.float32,
    )
    summed = lax.psum(partial_blocks, "col")
    factor = float(BLK * width_x * width_y * depth_z * lax.axis_size("col")) ** (-0.5)
    potential_blocks = (summed * factor).astype(jnp.bfloat16)
    block_total = hmask.shape[0]
    blocks_wide = block_total // lax.axis_size("col")
    row_start = lax.axis_index("row") * blocks_here
    col_start = lax.axis_index("col") * blocks_wide
    hpattern = lax.dynamic_slice(hmask, (row_start, col_start), (blocks_here, blocks_wide))
    ppattern = lax.dynamic_slice(pmask, (row_start, col_start), (blocks_here, blocks_wide))
    masked_h = (
        hamiltonian.reshape(blocks_here, BLK, blocks_wide, BLK)
        * hpattern[:, None, :, None].astype(jnp.bfloat16)
    ).reshape(blocks_here * BLK, blocks_wide * BLK)
    masked_p = (
        density.reshape(2, blocks_here, BLK, blocks_wide, BLK)
        * ppattern[None, :, None, :, None].astype(jnp.bfloat16)
    ).reshape(2, blocks_here * BLK, blocks_wide * BLK)

    def diagonal_term(operand):
        local = jnp.einsum(
            "kab,skbc->skac",
            potential_blocks,
            operand.reshape(2, blocks_here, BLK, operand.shape[2]),
            preferred_element_type=jnp.float32,
        )
        return local.reshape(2, blocks_here * BLK, operand.shape[2])

    def apply(operand):
        column_whole = lax.all_gather(operand, "row", axis=1, tiled=True)
        remote = jnp.einsum(
            "rk,skc->src",
            lax.all_gather(masked_h, "col", axis=1, tiled=True),
            column_whole,
            preferred_element_type=jnp.float32,
        )
        return remote + diagonal_term(operand)

    first = apply(masked_p)
    first_rounded = first.astype(jnp.bfloat16)
    second = apply(first_rounded)
    base = masked_p.astype(jnp.float32)
    half_square = 0.5 * TIME_STEP * TIME_STEP
    real_part = base[0] + TIME_STEP * first[1] - half_square * second[0]
    imag_part = base[1] - TIME_STEP * first[0] - half_square * second[1]
    stacked = jnp.stack([real_part, imag_part]).reshape(2, blocks_here, BLK, blocks_wide, BLK)
    stacked = stacked * ppattern[None, :, None, :, None].astype(jnp.float32)
    return stacked.reshape(2, blocks_here * BLK, blocks_wide * BLK).astype(jnp.bfloat16)


def solution(mesh):
    in_specs = (
        P("row", "col", None),
        P("row", "col", None, None),
        P("row", "col"),
        P(None, "row", "col"),
        P(),
        P(),
    )
    out_specs = P(None, "row", "col")
    return jax.shard_map(shards, mesh=mesh, in_specs=in_specs, out_specs=out_specs, check_vma=False)
```

profile of v0, /device:TPU:1, one launch (start us, length us, event | category | flops | bytes accessed | tf_op | source)
XLA Modules:
  0.0 729.8 jit_solution(5748484860902074060)
XLA Ops:
  6.5 0.0 all-reduce.3.cloned.1.call-start
  6.5 0.7 fusion.37
  7.3 4.3 collective-permute-start.1
  11.6 1.3 collective-permute-start
  12.9 0.0 collective-permute-done.1
  12.9 0.7 constant_dynamic-update-slice_fusion.1
  13.7 2.5 collective-permute-done
  16.2 3.8 collective-permute-start.2
  20.1 7.8 %collective-permute-start.3 = (f32[4,1,512]{2,1,0:T(1,128)S(1)}, f32[4,1,512]{2,1,0:T(1,128)S(1)}, u32[]{:S(2)}, u32[]{:S(2)}) collective-permute-start(f32[4,1,512]{2,1,0:T(1,128)S(1)} %get-tuple-element.9), channel_id=1, source_target_pairs={{0,1},{1,2},{2,3},{3,4},{4,5},{5,6},{6,7},{7,8},{8,9},{9,10},{10,1... | collective-permute-start | bytes 24584 | tf_op jit(solution)/shard_map/ppermute | solution.py:16
  27.9 0.8 dynamic-slice_convert_fusion.1
  28.7 0.0 collective-permute-done.2
  28.7 0.0 collective-permute-done.3
  28.7 0.1 select_maximum_fusion
  28.8 0.9 fusion.29
  29.7 0.0 copy-start
  29.7 2.7 multiply_convert_fusion
  32.5 0.1 copy-done
  32.6 1.7 convolution_bitcast_fusion.2
  34.2 0.0 all-reduce.3.cloned.1.call-update
  34.2 0.0 all-gather.6.cloned.1.call-start
  34.3 0.2 mul.100
  34.5 0.0 copy-done.5
  34.5 0.8 bitcast_multiply_fusion
  35.3 0.0 all-gather.6.cloned.1.call-update
  35.3 0.0 all-gather.4.cloned.1.call-start
  35.3 0.2 mul.96
  35.6 0.0 copy-done.2
  35.6 0.9 fusion.35
  36.5 0.0 all-gather.4.cloned.1.call-update
  36.6 0.0 all-gather.8.cloned.1.call-start
  36.6 0.1 broadcast_bitcast_fusion
  36.7 175.1 %all-reduce.3.cloned.1.call-done = f32[3,128,128]{2,1,0:T(8,128)} async-done(((f32[3,128,128]{2,1,0:T(8,128)}), f32[3,128,128]{2,1,0:T(8,128)}) %all-reduce.3.cloned.1.call-update) | async-done | bytes 196624 | tf_op jit(solution)/shard_map/psum | solution.py:40
  211.8 1.2 convolution_bitcast_fusion.1
  213.1 0.1 copy.18
  213.2 82.5 %all-gather.6.cloned.1.call-done = bf16[384,6144]{1,0:T(8,128)(2,1)} async-done(((bf16[384,384]{1,0:T(8,128)(2,1)}), bf16[384,6144]{1,0:T(8,128)(2,1)}) %all-gather.6.cloned.1.call-update) | async-done | bytes 4718608 | tf_op jit(solution)/shard_map/all_gather | solution.py:71
  295.7 203.1 %all-gather.4.cloned.1.call-done = bf16[2,6144,384]{2,1,0:T(8,128)(2,1)} async-done(((bf16[2,384,384]{2,1,0:T(8,128)(2,1)}), bf16[2,6144,384]{2,1,0:T(8,128)(2,1)}) %all-gather.4.cloned.1.call-update) | async-done | bytes 9437200 | tf_op jit(solution)/shard_map/all_gather | solution.py:68
  498.8 10.2 %fusion.38 = (bf16[2,384,384]{2,1,0:T(8,128)(2,1)}, f32[2,384,384]{2,1,0:T(8,128)}) fusion(f32[2,384,384]{2,1,0:T(8,128)S(1)} %bitcast.74, bf16[2,6144,384]{2,1,0:T(8,128)(2,1)} %all-gather.4.cloned.1.call-done, bf16[384,6144]{1,0:T(8,128)(2,1)} %all-gather.6.cloned.1.call-done), kind=kOutput, calls=%fused_computation.61 | convolution fusion | flops 3624468480 | bytes 17104896 | tf_op jit(solution)/shard_map/rk,skc->src/dot_general | solution.py:69
  508.9 0.0 all-gather.8.cloned.1.call-update
  509.0 0.2 mul.119
  509.1 0.1 copy.41
  509.2 0.0 copy-done.4
  509.2 0.8 copy-done.1
  510.0 0.3 convolution_bitcast_fusion
  510.3 0.1 copy.22
  510.4 203.2 %all-gather.8.cloned.1.call-done = bf16[2,6144,384]{2,1,0:T(8,128)(2,1)} async-done(((bf16[2,384,384]{2,1,0:T(8,128)(2,1)}), bf16[2,6144,384]{2,1,0:T(8,128)(2,1)}) %all-gather.8.cloned.1.call-update) | async-done | bytes 9437200 | tf_op jit(solution)/shard_map/all_gather | solution.py:68
  713.6 8.5 %fusion.13 = f32[2,384,384]{2,1,0:T(8,128)S(1)} fusion(f32[2,384,384]{2,1,0:T(8,128)S(1)} %bitcast.75, bf16[2,6144,384]{2,1,0:T(8,128)(2,1)} %all-gather.8.cloned.1.call-done, bf16[384,6144]{1,0:T(8,128)(2,1)} %all-gather.6.cloned.1.call-done), kind=kOutput, calls=%fused_computation.10 | convolution fusion | flops 3624173568 | bytes 16515072 | tf_op jit(solution)/shard_map/rk,skc->src/dot_general | solution.py:69
  722.1 0.3 fusion.19
  722.4 0.9 fusion.16
  (11 shorter events, 0.1 us)
Async XLA Ops:
  6.5 205.3 %all-reduce.3.cloned.1.call-start = ((), (), s32[]{:S(2)}) async-start(), calls=%async_computation.2 | async-start | bytes 393216 | tf_op jit(solution)/shard_map/psum | solution.py:40
  7.3 5.7 collective-permute-start.1
  11.6 4.6 collective-permute-start
  16.2 12.5 %collective-permute-start.2 = (f32[4,1,512]{2,1,0:T(1,128)S(1)}, f32[4,1,512]{2,1,0:T(1,128)S(1)}, u32[]{:S(2)}, u32[]{:S(2)}) collective-permute-start(f32[4,1,512]{2,1,0:T(1,128)S(1)} %get-tuple-element.10), channel_id=1, source_target_pairs={{1,0},{2,1},{3,2},{4,3},{5,4},{6,5},{7,6},{8,7},{9,8},{10,9},{11,1... | collective-permute-start | bytes 24584 | tf_op jit(solution)/shard_map/ppermute | solution.py:19
  20.1 8.6 %collective-permute-start.3 = (f32[4,1,512]{2,1,0:T(1,128)S(1)}, f32[4,1,512]{2,1,0:T(1,128)S(1)}, u32[]{:S(2)}, u32[]{:S(2)}) collective-permute-start(f32[4,1,512]{2,1,0:T(1,128)S(1)} %get-tuple-element.9), channel_id=1, source_target_pairs={{0,1},{1,2},{2,3},{3,4},{4,5},{5,6},{6,7},{7,8},{8,9},{9,10},{10,1... | collective-permute-start | bytes 24584 | tf_op jit(solution)/shard_map/ppermute | solution.py:16
  29.7 2.8 copy-start
  32.6 1.9 copy-start.5
  32.6 3.0 copy-start.2
  34.2 261.5 %all-gather.6.cloned.1.call-start = ((), (), s32[]{:S(2)}) async-start(), calls=%async_computation.1 | async-start | bytes 5013504 | tf_op jit(solution)/shard_map/all_gather | solution.py:71
  35.3 463.5 %all-gather.4.cloned.1.call-start = ((), (), s32[]{:S(2)}) async-start(), calls=%async_computation | async-start | bytes 10027008 | tf_op jit(solution)/shard_map/all_gather | solution.py:68
  36.6 677.0 %all-gather.8.cloned.1.call-start = ((), (), s32[]{:S(2)}) async-start(), calls=%async_computation.3 | async-start | bytes 10027008 | tf_op jit(solution)/shard_map/all_gather | solution.py:68
  498.8 10.4 %copy-start.4 = (f32[3,128,128]{2,1,0:T(8,128)S(1)}, f32[3,128,128]{2,1,0:T(8,128)}, u32[]{:S(2)}) copy-start(f32[3,128,128]{2,1,0:T(8,128)} %all-reduce.3.cloned.1.call-done) | copy-start | bytes 589828
  508.9 1.1 copy-start.1
  713.6 8.5 %copy-start.3 = (f32[2,384,384]{2,1,0:T(8,128)S(1)}, f32[2,384,384]{2,1,0:T(8,128)}, u32[]{:S(2)}) copy-start(f32[2,384,384]{2,1,0:T(8,128)} %get-tuple-element.16) | copy-start | bytes 3538948
Sparse Core Ops, SparseCore 0:
  34.4 177.4 all-reduce.2
  214.4 81.2 all-gather.5
  297.5 201.2 all-gather.3
  509.1 204.4 all-gather.7
where the time goes:
time: 730 us
  waiting for transfers between devices  667 us (91%)
  matrix products  21.9 us (3%)
  starting transfers between devices  17.4 us (2%)
  between operations  13.3 us (2%)
  other arithmetic  7.46 us (1%)
    all_gather x2, waiting for transfers between devices, apply(): column_whole = lax.all_gather(operand, 'row', axis=1, tiled=True)  406 us
    psum x1, waiting for transfers between devices, shards(): summed = lax.psum(partial_blocks, 'col')  175 us
    all_gather x1, waiting for transfers between devices, apply(): lax.all_gather(masked_h, 'col', axis=1, tiled=True)  82.5 us
    dot_general x2, matrix products, apply(): jnp.einsum('rk,skc->src', lax.all_gather(masked_h, 'col', axis=1, tiled=T...  18.7 us
  transfers between devices with their start and end apart: 8, of which 5 were waited for; matrix products, arithmetic and copies ran while one was open for 1% of the time, Pallas kernels for 0%

commit v1 on v0

--- a/solution.py
+++ b/solution.py
@@ -37,7 +37,7 @@
         basis.reshape(width_x, width_y, blocks_here, BLK, depth_z),
         preferred_element_type=jnp.float32,
     )
-    summed = lax.psum(partial_blocks, "col")
+    summed = jnp.sum(lax.all_gather(partial_blocks, "col"), axis=0)
     factor = float(BLK * width_x * width_y * depth_z * lax.axis_size("col")) ** (-0.5)
     potential_blocks = (summed * factor).astype(jnp.bfloat16)
     block_total = hmask.shape[0]

time: 730 us -> 626 us (0.86)
  waiting for transfers between devices: 667 us -> 561 us
    psum x1 -> x0, waiting for transfers between devices: 175 us -> none  [shards(): summed = lax.psum(partial_blocks, 'col')]
    all_gather x0 -> x1, waiting for transfers between devices: none -> 74.1 us  [shards(): summed = jnp.sum(lax.all_gather(partial_blocks, 'col'), axis=0)]
  transfers between devices with their start and end apart: 8 -> 8, of which waited for: 5 -> 6; matrix products, arithmetic and copies ran while one was open for 1% -> 1% of each run, Pallas kernels for 0% -> 0%
where the time goes in v1:
time: 626 us
  waiting for transfers between devices  561 us (90%)
  matrix products  20.9 us (3%)
  starting transfers between devices  17.4 us (3%)
  between operations  13.3 us (2%)
  other arithmetic  9.49 us (2%)
    all_gather x2, waiting for transfers between devices, apply(): column_whole = lax.all_gather(operand, 'row', axis=1, tiled=True)  406 us
    all_gather x1, waiting for transfers between devices, apply(): lax.all_gather(masked_h, 'col', axis=1, tiled=True)  77.5 us
    all_gather x1, waiting for transfers between devices, shards(): summed = jnp.sum(lax.all_gather(partial_blocks, 'col'), axis=0)  74.1 us
    dot_general x2, matrix products, apply(): jnp.einsum('rk,skc->src', lax.all_gather(masked_h, 'col', axis=1, tiled=T...  18.6 us
  transfers between devices with their start and end apart: 8, of which 6 were waited for; matrix products, arithmetic and copies ran while one was open for 1% of the time, Pallas kernels for 0%

profile of v1, /device:TPU:1, one launch (start us, length us, event | category | flops | bytes accessed | tf_op | source)
XLA Modules:
  0.0 625.6 jit_solution(3958333334108763658)
XLA Ops:
  6.5 0.0 all-gather.12.cloned.1.call-start
  6.5 0.7 fusion.37
  7.3 4.3 collective-permute-start.1
  11.6 1.3 collective-permute-start
  12.9 0.0 collective-permute-done.1
  12.9 0.7 constant_dynamic-update-slice_fusion.1
  13.7 2.5 collective-permute-done
  16.2 3.8 collective-permute-start.2
  20.1 7.8 %collective-permute-start.3 = (f32[4,1,512]{2,1,0:T(1,128)S(1)}, f32[4,1,512]{2,1,0:T(1,128)S(1)}, u32[]{:S(2)}, u32[]{:S(2)}) collective-permute-start(f32[4,1,512]{2,1,0:T(1,128)S(1)} %get-tuple-element.9), channel_id=1, source_target_pairs={{0,1},{1,2},{2,3},{3,4},{4,5},{5,6},{6,7},{7,8},{8,9},{9,10},{10,1... | collective-permute-start | bytes 24584 | tf_op jit(solution)/shard_map/ppermute | solution.py:16
  27.9 0.0 collective-permute-done.2
  27.9 0.8 collective-permute-done.3
  28.6 0.1 select_maximum_fusion
  28.8 0.9 fusion.29
  29.7 0.0 copy-start
  29.7 2.7 multiply_convert_fusion
  32.4 0.1 copy-done
  32.5 1.7 convolution_bitcast_fusion.2
  34.2 0.0 all-gather.12.cloned.1.call-update
  34.2 0.0 all-gather.8.cloned.1.call-start
  34.3 0.8 dynamic-slice_convert_fusion.1
  35.1 0.2 mul.100
  35.2 0.0 copy-done.4
  35.2 0.8 bitcast_multiply_fusion
  36.0 0.0 all-gather.8.cloned.1.call-update
  36.0 0.0 all-gather.6.cloned.1.call-start
  36.1 0.2 mul.96
  36.3 0.0 copy-done.2
  36.3 0.9 fusion.35
  37.3 0.0 all-gather.6.cloned.1.call-update
  37.3 0.0 all-gather.10.cloned.1.call-start
  37.3 0.1 broadcast_bitcast_fusion
  37.4 74.1 %all-gather.12.cloned.1.call-done = f32[48,128,128]{2,1,0:T(8,128)} async-done(((f32[3,128,128]{2,1,0:T(8,128)}), f32[48,128,128]{2,1,0:T(8,128)}) %all-gather.12.cloned.1.call-update) | async-done | bytes 3145744 | tf_op jit(solution)/shard_map/all_gather | solution.py:40
  111.6 2.1 reduce_sum.9
  113.6 0.3 convolution_bitcast_fusion.1
  113.9 0.1 copy.24
  114.0 77.5 %all-gather.8.cloned.1.call-done = bf16[384,6144]{1,0:T(8,128)(2,1)} async-done(((bf16[384,384]{1,0:T(8,128)(2,1)}), bf16[384,6144]{1,0:T(8,128)(2,1)}) %all-gather.8.cloned.1.call-update) | async-done | bytes 4718608 | tf_op jit(solution)/shard_map/all_gather | solution.py:71
  191.5 203.1 %all-gather.6.cloned.1.call-done = bf16[2,6144,384]{2,1,0:T(8,128)(2,1)} async-done(((bf16[2,384,384]{2,1,0:T(8,128)(2,1)}), bf16[2,6144,384]{2,1,0:T(8,128)(2,1)}) %all-gather.6.cloned.1.call-update) | async-done | bytes 9437200 | tf_op jit(solution)/shard_map/all_gather | solution.py:68
  394.5 10.1 %fusion.38 = (bf16[2,384,384]{2,1,0:T(8,128)(2,1)}, f32[2,384,384]{2,1,0:T(8,128)}) fusion(f32[2,384,384]{2,1,0:T(8,128)S(1)} %bitcast.76, bf16[2,6144,384]{2,1,0:T(8,128)(2,1)} %all-gather.6.cloned.1.call-done, bf16[384,6144]{1,0:T(8,128)(2,1)} %all-gather.8.cloned.1.call-done), kind=kOutput, calls=%fused_computation.61 | convolution fusion | flops 3624468480 | bytes 17104896 | tf_op jit(solution)/shard_map/rk,skc->src/dot_general | solution.py:69
  404.7 0.0 all-gather.10.cloned.1.call-update
  404.7 0.2 mul.119
  404.9 0.1 copy.45
  404.9 0.8 copy-done.1
  405.7 0.3 convolution_bitcast_fusion
  406.0 0.1 copy.28
  406.1 203.2 %all-gather.10.cloned.1.call-done = bf16[2,6144,384]{2,1,0:T(8,128)(2,1)} async-done(((bf16[2,384,384]{2,1,0:T(8,128)(2,1)}), bf16[2,6144,384]{2,1,0:T(8,128)(2,1)}) %all-gather.10.cloned.1.call-update) | async-done | bytes 9437200 | tf_op jit(solution)/shard_map/all_gather | solution.py:68
  609.3 8.5 %fusion.13 = f32[2,384,384]{2,1,0:T(8,128)S(1)} fusion(f32[2,384,384]{2,1,0:T(8,128)S(1)} %bitcast.77, bf16[2,6144,384]{2,1,0:T(8,128)(2,1)} %all-gather.10.cloned.1.call-done, bf16[384,6144]{1,0:T(8,128)(2,1)} %all-gather.8.cloned.1.call-done), kind=kOutput, calls=%fused_computation.10 | convolution fusion | flops 3624173568 | bytes 16515072 | tf_op jit(solution)/shard_map/rk,skc->src/dot_general | solution.py:69
  617.8 0.3 fusion.19
  618.1 0.9 fusion.16
  (10 shorter events, 0.1 us)
Async XLA Ops:
  6.5 105.0 %all-gather.12.cloned.1.call-start = ((), (), s32[]{:S(2)}) async-start(), calls=%async_computation.3 | async-start | bytes 3342336 | tf_op jit(solution)/shard_map/all_gather | solution.py:40
  7.3 5.7 collective-permute-start.1
  11.6 4.6 collective-permute-start
  16.2 11.7 %collective-permute-start.2 = (f32[4,1,512]{2,1,0:T(1,128)S(1)}, f32[4,1,512]{2,1,0:T(1,128)S(1)}, u32[]{:S(2)}, u32[]{:S(2)}) collective-permute-start(f32[4,1,512]{2,1,0:T(1,128)S(1)} %get-tuple-element.10), channel_id=1, source_target_pairs={{1,0},{2,1},{3,2},{4,3},{5,4},{6,5},{7,6},{8,7},{9,8},{10,9},{11,1... | collective-permute-start | bytes 24584 | tf_op jit(solution)/shard_map/ppermute | solution.py:19
  20.1 8.6 %collective-permute-start.3 = (f32[4,1,512]{2,1,0:T(1,128)S(1)}, f32[4,1,512]{2,1,0:T(1,128)S(1)}, u32[]{:S(2)}, u32[]{:S(2)}) collective-permute-start(f32[4,1,512]{2,1,0:T(1,128)S(1)} %get-tuple-element.9), channel_id=1, source_target_pairs={{0,1},{1,2},{2,3},{3,4},{4,5},{5,6},{6,7},{7,8},{8,9},{9,10},{10,1... | collective-permute-start | bytes 24584 | tf_op jit(solution)/shard_map/ppermute | solution.py:16
  29.7 2.8 copy-start
  32.5 2.7 copy-start.4
  32.5 3.8 copy-start.2
  34.2 157.3 %all-gather.8.cloned.1.call-start = ((), (), s32[]{:S(2)}) async-start(), calls=%async_computation.1 | async-start | bytes 5013504 | tf_op jit(solution)/shard_map/all_gather | solution.py:71
  36.0 358.5 %all-gather.6.cloned.1.call-start = ((), (), s32[]{:S(2)}) async-start(), calls=%async_computation | async-start | bytes 10027008 | tf_op jit(solution)/shard_map/all_gather | solution.py:68
  37.3 572.0 %all-gather.10.cloned.1.call-start = ((), (), s32[]{:S(2)}) async-start(), calls=%async_computation.2 | async-start | bytes 10027008 | tf_op jit(solution)/shard_map/all_gather | solution.py:68
  404.7 1.1 copy-start.1
  609.3 8.5 %copy-start.3 = (f32[2,384,384]{2,1,0:T(8,128)S(1)}, f32[2,384,384]{2,1,0:T(8,128)}, u32[]{:S(2)}) copy-start(f32[2,384,384]{2,1,0:T(8,128)} %get-tuple-element.16) | copy-start | bytes 3538948
Sparse Core Ops, SparseCore 0:
  34.3 77.1 all-gather.11
  114.1 77.3 all-gather.7
  193.3 201.2 all-gather.5
  404.8 204.4 all-gather.9
